TPU v7x, 32 devices: a whole 2x2x4 slice. The times are simulated.
32 devices in a mesh: groups: 2 (over x), dev: 16 (over z, y, core).
Axes of the slice: x: 2, y: 2, z: 4, core: 2. Of those that a mesh axis runs over, the one named last changes fastest.
Arguments:
- queries: bfloat16 [2, 32, 128, 1024], P(None, ('groups', 'dev')), parts along dimension 1, may hold values from -180 to 180
- keys_values: bfloat16 [2, 32, 2, 1664, 128], P(None, ('groups', 'dev')), parts along dimension 1, may hold values from -6 to 6
- residual: bfloat16 [2, 2048, 2048], P(None, ('groups', 'dev')), parts along dimension 1, may hold values from -6 to 6
- norm_gain: float32 [2048], replicated, may hold values from 0.1 to 1.9
- gate_up: bfloat16 [16, 2048, 1536], P('dev'), may hold values from -0.125 to 0.125
- down_proj: bfloat16 [16, 768, 2048], P('dev'), may hold values from -0.21875 to 0.21875
- expert_ids: int32 [2, 2048, 8], P(None, ('groups', 'dev')), parts along dimension 1, may hold values from 0 to 15, all different within a row; in each aligned block of 64 rows (0 to 63, 64 to 127, ..., all dimensions but the last counted through in order) at most 40 rows name the same one
- expert_gates: int32 [2, 2048, 8], P(None, ('groups', 'dev')), parts along dimension 1, may hold values from 1 to 1023
Outputs:
- layer_out: bfloat16 [2, 2048, 2048], P(None, ('groups', 'dev')), parts along dimension 1
There are 2 independent parts, one for each index of `groups`. A program takes and returns all parts, laid end to end along the dimension named above; an argument that names none is the same for every part. Nothing has to cross between parts.
Inputs may be any that keep to these rules, and one draw needn't show every extreme that they name: `expert_ids`: in each micro-batch and each aligned block of 64 rows (the tokens of one device), no expert is named by more than 40 rows, a bound that some block reaches; the 8 experts of a row differ.
All inputs are finite; a program needn't handle non-finite values.
Results may differ from a plain program's by a relative error of at most 0.0039.
Values may be sent and summed in bfloat16 or wider, within the bound.
A program may use at most 128 MiB of HBM per device.

v0:
```python
import math
import jax
import jax.numpy as jnp
from jax import lax
from jax.sharding import PartitionSpec as P


def attend(query_rows, cached_pairs):
    batches, length, feat_width = query_rows.shape
    context = cached_pairs.shape[2]
    head_size = cached_pairs.shape[3]
    groups = feat_width // head_size
    head_rows = query_rows.reshape(batches, length, groups, head_size)
    scores = jnp.einsum(
        "mqgd,mkd->mgqk", head_rows, cached_pairs[:, 0], preferred_element_type=jnp.float32
    ) / math.sqrt(head_size)
    query_pos = context - length + lax.broadcasted_iota(jnp.int32, (length, context), 0)
    key_pos = lax.broadcasted_iota(jnp.int32, (length, context), 1)
    allowed = key_pos <= query_pos
    scores = jnp.where(allowed, scores, -1e30)
    highest = jnp.max(scores, axis=-1, keepdims=True)
    scaled_exp = jnp.where(allowed, jnp.exp(scores - highest), 0.0)
    totals = jnp.sum(scaled_exp, axis=-1, keepdims=True)
    weights = (scaled_exp / totals).astype(jnp.bfloat16)
    blended = jnp.einsum(
        "mgqk,mkd->mqgd", weights, cached_pairs[:, 1], preferred_element_type=jnp.float32
    )
    return blended.astype(jnp.bfloat16).reshape(batches, length, feat_width)


def to_owners(exchanged, kv_heads):
    batches, sources, positions, feat_width = exchanged.shape
    grouped = exchanged.reshape(batches, sources // kv_heads, kv_heads, positions, feat_width)
    grouped = jnp.transpose(grouped, (0, 1, 3, 2, 4))
    return grouped.reshape(batches, sources // kv_heads * positions, kv_heads * feat_width)


def prepare(attn_rows, residual, norm_gain):
    stream = residual.astype(jnp.float32) + attn_rows.astype(jnp.float32)
    meansq = jnp.mean(stream * stream, axis=-1, keepdims=True)
    normed = (stream * lax.rsqrt(meansq + 1e-06) * norm_gain).astype(jnp.bfloat16)
    return (stream, normed)


def dense_shares(expert_ids, expert_gates, experts):
    shares = expert_gates.astype(jnp.float32)
    shares = shares / jnp.sum(shares, axis=-1, keepdims=True)
    named = expert_ids[..., None] == jnp.arange(experts, dtype=jnp.int32)
    return jnp.sum(jnp.where(named, shares[..., None], 0.0), axis=-2)


def run_expert(rows_in, gate_up, down_proj, weight):
    hidden_width = down_proj.shape[1]
    projected = jnp.dot(rows_in, gate_up[0], preferred_element_type=jnp.float32)
    hidden = (jax.nn.silu(projected[:, :hidden_width]) * projected[:, hidden_width:]).astype(
        jnp.bfloat16
    )
    output = jnp.dot(hidden, down_proj[0], preferred_element_type=jnp.float32)
    return (output * weight).astype(jnp.bfloat16)


def body(queries, keys_values, residual, norm_gain, gate_up, down_proj, expert_ids, expert_gates):
    devices = lax.axis_size("dev")
    me = lax.axis_index("dev")
    model_width = residual.shape[2]
    kv_heads = model_width // queries.shape[3]
    experts = devices * gate_up.shape[0]
    own_query = queries[:, 0]
    own_pairs = keys_values[:, 0]
    batches, length, feat_width = own_query.shape
    positions = length // devices
    weights = dense_shares(expert_ids, expert_gates, experts)
    weights = lax.all_gather(weights, "dev", axis=1, tiled=True)
    mine = jnp.sum(
        jnp.where(jnp.arange(experts, dtype=jnp.int32) == me, weights, 0.0), axis=-1, keepdims=True
    )
    pieces = []
    for batch_index in range(batches):
        window = slice(batch_index, batch_index + 1)
        blended_heads = attend(own_query[window], own_pairs[window])
        outgoing_rows = blended_heads.reshape(1, devices, positions, feat_width)
        arrived_rows = lax.all_to_all(outgoing_rows, "dev", split_axis=1, concat_axis=1, tiled=True)
        attn_rows = to_owners(arrived_rows, kv_heads)
        stream, normed = prepare(attn_rows[0], residual[batch_index], norm_gain)
        rows_in = lax.all_gather(normed, "dev", axis=0, tiled=True)
        partial = run_expert(rows_in, gate_up, down_proj, mine[batch_index])
        summed = lax.psum_scatter(partial, "dev", scatter_dimension=0, tiled=True)
        pieces.append((stream + summed.astype(jnp.float32)).astype(jnp.bfloat16))
    return jnp.stack(pieces, axis=0)


def solution(mesh):
    in_specs = (
        P(None, ("groups", "dev"), None, None),
        P(None, ("groups", "dev"), None, None, None),
        P(None, ("groups", "dev"), None),
        P(),
        P("dev", None, None),
        P("dev", None, None),
        P(None, ("groups", "dev"), None),
        P(None, ("groups", "dev"), None),
    )
    out_specs = P(None, ("groups", "dev"), None)
    return jax.shard_map(body, mesh=mesh, in_specs=in_specs, out_specs=out_specs, check_vma=False)
```

profile of v0, /device:TPU:0, one launch (start us, length us, event | category | flops | bytes accessed | tf_op | source)
XLA Modules:
  0.0 324.2 jit_solution(8820558559050557088)
XLA Ops:
  6.5 0.1 iota_compare_fusion
  6.7 2.9 slice_bitcast_fusion
  9.6 1.8 fusion.50
  11.4 1.8 copy.62
  13.2 1.8 copy.64
  15.0 2.3 fusion.4
  17.3 2.8 fusion.6
  20.1 1.6 fusion.7
  21.7 2.6 fusion.26
  24.3 0.9 copy.55
  25.2 1.8 reshape_reshape.7
  26.9 7.5 %all-to-all-start.1 = ((bf16[1,16,8,1024]{3,2,0,1:T(8,128)(2,1)}), bf16[1,16,8,1024]{3,2,0,1:T(8,128)(2,1)}, u32[]{:S(2)}, u32[]{:S(2)}) async-start(bf16[1,16,8,1024]{3,2,0,1:T(8,128)(2,1)} %bitcast.156), calls=%async_computation.2 | async-start | bytes 524288 | tf_op jit(solution)/shard_map/all_to_all | solution.py:82
  34.4 0.0 copy-start.5
  34.4 5.5 %fusion.29 = bf16[1,128,8,128]{3,1,2,0:T(8,128)(2,1)S(1)} fusion(f32[8,128]{1,0:T(8,128)S(1)} %get-tuple-element.7, f32[8,128]{1,0:T(8,128)S(1)} %get-tuple-element.19, f32[1664,128,8]{1,0,2:T(8,128)} %copy-done.1, pred[128,1664]{0,1:T(8,128)(4,1)S(1)} %iota_compare_fusion, bf16[1,2,1664,128]{3,2,1,0:T(8,128)(2,1)} %get-tuple-element.10), kind=kOutput, calls=%fused_computation.31 | convolution fusion | flops 446562304 | bytes 7725056 | tf_op jit(solution)/shard_map/mgqk,mkd->mqgd/dot_general | solution.py:25
  39.9 0.0 copy-start.7
  40.0 0.0 copy-start.6
  40.0 0.2 copy.48
  40.2 0.8 reshape_reshape.6
  41.0 3.5 %all-to-all-done.1 = bf16[1,16,8,1024]{3,2,0,1:T(8,128)(2,1)} async-done(((bf16[1,16,8,1024]{3,2,0,1:T(8,128)(2,1)}), bf16[1,16,8,1024]{3,2,0,1:T(8,128)(2,1)}, u32[]{:S(2)}, u32[]{:S(2)}) %all-to-all-start.1) | async-done | bytes 262176 | tf_op jit(solution)/shard_map/all_to_all | solution.py:82
  44.5 3.5 %all-to-all-start = ((bf16[1,16,8,1024]{3,2,0,1:T(8,128)(2,1)}), bf16[1,16,8,1024]{3,2,0,1:T(8,128)(2,1)S(1)}, u32[]{:S(2)}, u32[]{:S(2)}) async-start(bf16[1,16,8,1024]{3,2,0,1:T(8,128)(2,1)} %bitcast.157), calls=%async_computation | async-start | bytes 524288 | tf_op jit(solution)/shard_map/all_to_all | solution.py:82
  48.0 0.2 all-gather.5.cloned.1.call-start
  48.3 1.8 convert.11
  50.1 7.9 %all-to-all-done = bf16[1,16,8,1024]{3,2,0,1:T(8,128)(2,1)S(1)} async-done(((bf16[1,16,8,1024]{3,2,0,1:T(8,128)(2,1)}), bf16[1,16,8,1024]{3,2,0,1:T(8,128)(2,1)S(1)}, u32[]{:S(2)}, u32[]{:S(2)}) %all-to-all-start) | async-done | bytes 262176 | tf_op jit(solution)/shard_map/all_to_all | solution.py:82
  58.1 1.6 multiply_reduce_fusion.1
  59.7 2.2 multiply_convert_fusion.3
  61.9 0.0 all-gather.5.cloned.1.call-update
  61.9 0.0 all-gather.3.cloned.1.call-start
  62.0 0.7 all-gather.3.cloned.1.call-update
  62.7 0.0 reduce-scatter.5.cloned.1.call-start
  62.7 0.1 convert_divide_fusion
  62.8 0.1 copy.50
  62.9 24.2 %all_gather.10 = f32[2,1024,16]{2,0,1:T(2,128)S(1)} all-gather(f32[2,64,16]{2,0,1:T(2,128)S(1)} %copy.50), channel_id=1, replica_groups=mesh['groups'=2,'dev'=16] {'dev'}, dimensions={1}, use_global_device_ids=true | all-gather | bytes 139264 | tf_op jit(solution)/shard_map/all_gather | solution.py:73
  87.1 1.2 select_reduce_fusion
  88.3 1.1 fusion.49
  89.4 1.3 copy.65
  90.7 22.6 %all-gather.5.cloned.1.call-done = bf16[1024,2048]{1,0:T(8,128)(2,1)} async-done(((bf16[64,2048]{1,0:T(8,128)(2,1)}), bf16[1024,2048]{1,0:T(8,128)(2,1)}) %all-gather.5.cloned.1.call-update) | async-done | bytes 4194320 | tf_op jit(solution)/shard_map/all_gather | solution.py:85
  113.3 10.0 %fusion = f32[1024,1536]{1,0:T(8,128)S(1)} fusion(bf16[1024,2048]{1,0:T(8,128)(2,1)} %all-gather.5.cloned.1.call-done, bf16[1,2048,1536]{2,1,0:T(8,128)(2,1)} %param.12), kind=kOutput, calls=%fused_computation.8 | convolution fusion | flops 6442450944 | bytes 16777216 | tf_op jit(solution)/shard_map/dot_general | solution.py:54
  123.4 5.1 %multiply_convert_fusion = bf16[1024,2048]{1,0:T(8,128)(2,1)} fusion(f32[1024]{0:T(1024)S(1)} %bitcast.159, bf16[1,768,2048]{2,1,0:T(8,128)(2,1)S(1)} %copy-done, f32[1024,1536]{1,0:T(8,128)S(1)} %fusion), kind=kOutput, calls=%fused_computation | convolution fusion | flops 3230138368 | bytes 13635584 | tf_op jit(solution)/shard_map/dot_general | solution.py:58
  128.4 0.0 reduce-scatter.5.cloned.1.call-update
  128.5 0.0 reduce-scatter.3.cloned.1.call-start
  128.5 1.2 copy.63
  129.7 34.7 %all-gather.3.cloned.1.call-done = bf16[1024,2048]{1,0:T(8,128)(2,1)} async-done(((bf16[64,2048]{1,0:T(8,128)(2,1)}), bf16[1024,2048]{1,0:T(8,128)(2,1)}) %all-gather.3.cloned.1.call-update) | async-done | bytes 4194320 | tf_op jit(solution)/shard_map/all_gather | solution.py:85
  164.4 10.0 %fusion.2 = f32[1024,1536]{1,0:T(8,128)S(1)} fusion(bf16[1024,2048]{1,0:T(8,128)(2,1)} %all-gather.3.cloned.1.call-done, bf16[1,2048,1536]{2,1,0:T(8,128)(2,1)} %param.12), kind=kOutput, calls=%fused_computation.10 | convolution fusion | flops 6442450944 | bytes 16777216 | tf_op jit(solution)/shard_map/dot_general | solution.py:54
  174.4 5.1 %multiply_convert_fusion.1 = bf16[1024,2048]{1,0:T(8,128)(2,1)} fusion(f32[1024]{0:T(1024)S(1)} %bitcast.160, bf16[1,768,2048]{2,1,0:T(8,128)(2,1)S(1)} %copy-done, f32[1024,1536]{1,0:T(8,128)S(1)} %fusion.2), kind=kOutput, calls=%fused_computation.1 | convolution fusion | flops 3230138368 | bytes 13635584 | tf_op jit(solution)/shard_map/dot_general | solution.py:58
  179.5 0.0 reduce-scatter.3.cloned.1.call-update
  179.5 60.1 %reduce-scatter.5.cloned.1.call-done = bf16[64,2048]{1,0:T(8,128)(2,1)} async-done(((bf16[1024,2048]{1,0:T(8,128)(2,1)}), bf16[64,2048]{1,0:T(8,128)(2,1)}) %reduce-scatter.5.cloned.1.call-update) | async-done | bytes 262160 | tf_op jit(solution)/shard_map/reduce_scatter | solution.py:87
  239.6 75.5 %reduce-scatter.3.cloned.1.call-done = bf16[64,2048]{1,0:T(8,128)(2,1)} async-done(((bf16[1024,2048]{1,0:T(8,128)(2,1)}), bf16[64,2048]{1,0:T(8,128)(2,1)}) %reduce-scatter.3.cloned.1.call-update) | async-done | bytes 262160 | tf_op jit(solution)/shard_map/reduce_scatter | solution.py:87
  315.2 2.5 fusion.34
  (19 shorter events, 0.1 us)
Async XLA Ops:
  6.5 116.8 %copy-start = (bf16[1,768,2048]{2,1,0:T(8,128)(2,1)S(1)}, bf16[1,768,2048]{2,1,0:T(8,128)(2,1)}, u32[]{:S(2)}) copy-start(bf16[1,768,2048]{2,1,0:T(8,128)(2,1)} %param.13) | copy-start | bytes 9437188
  15.0 2.3 copy-start.3
  15.0 2.3 copy-start.4
  17.3 2.8 copy-start.1
  26.9 17.5 %all-to-all-start.1 = ((bf16[1,16,8,1024]{3,2,0,1:T(8,128)(2,1)}), bf16[1,16,8,1024]{3,2,0,1:T(8,128)(2,1)}, u32[]{:S(2)}, u32[]{:S(2)}) async-start(bf16[1,16,8,1024]{3,2,0,1:T(8,128)(2,1)} %bitcast.156), calls=%async_computation.2 | async-start | bytes 524288 | tf_op jit(solution)/shard_map/all_to_all | solution.py:82
  34.4 25.3 %copy-start.5 = (f32[2048]{0:T(1024)S(1)}, f32[2048]{0:T(1024)}, u32[]{:S(2)}) copy-start(f32[2048]{0:T(1024)} %param.11) | copy-start | bytes 24580
  39.9 22.8 %copy-start.7 = (s32[2,64,8]{1,2,0:T(8,128)S(1)}, s32[2,64,8]{1,2,0:T(8,128)}, u32[]{:S(2)}) copy-start(s32[2,64,8]{1,2,0:T(8,128)} %param.15) | copy-start | bytes 12292
  40.0 22.8 %copy-start.6 = (s32[2,64,8]{1,2,0:T(8,128)S(1)}, s32[2,64,8]{1,2,0:T(8,128)}, u32[]{:S(2)}) copy-start(s32[2,64,8]{1,2,0:T(8,128)} %param.14) | copy-start | bytes 12292
  44.5 13.5 %all-to-all-start = ((bf16[1,16,8,1024]{3,2,0,1:T(8,128)(2,1)}), bf16[1,16,8,1024]{3,2,0,1:T(8,128)(2,1)S(1)}, u32[]{:S(2)}, u32[]{:S(2)}) async-start(bf16[1,16,8,1024]{3,2,0,1:T(8,128)(2,1)} %bitcast.157), calls=%async_computation | async-start | bytes 524288 | tf_op jit(solution)/shard_map/all_to_all | solution.py:82
  48.0 65.3 %all-gather.5.cloned.1.call-start = ((), (), s32[]{:S(2)}) async-start(), calls=%async_computation.6 | async-start | bytes 4456448 | tf_op jit(solution)/shard_map/all_gather | solution.py:85
  58.1 1.7 copy-start.2
  61.9 102.5 %all-gather.3.cloned.1.call-start = ((), (), s32[]{:S(2)}) async-start(), calls=%async_computation.4 | async-start | bytes 4456448 | tf_op jit(solution)/shard_map/all_gather | solution.py:85
  62.7 177.0 %reduce-scatter.5.cloned.1.call-start = ((), (), s32[]{:S(2)}) async-start(), calls=%async_computation.7 | async-start | bytes 4456448 | tf_op jit(solution)/shard_map/reduce_scatter | solution.py:87
  128.5 186.7 %reduce-scatter.3.cloned.1.call-start = ((), (), s32[]{:S(2)}) async-start(), calls=%async_computation.5 | async-start | bytes 4456448 | tf_op jit(solution)/shard_map/reduce_scatter | solution.py:87
Sparse Core Ops, SparseCore 0:
  62.0 51.2 all-gather.4
  115.5 48.8 all-gather.2
  168.3 71.2 reduce-scatter.4
  243.3 71.7 reduce-scatter.2
where the time goes:
time: 325 us; the launch traced here: 324 us
  waiting for transfers between devices  205 us (63%)
  matrix products  43.3 us (13%)
  blocking collectives  24.2 us (7%)
  local copies, waits for them, and re-layouts  15.7 us (5%)
  between operations  13.4 us (4%)
  starting transfers between devices  11.3 us (3%)
  other arithmetic  11.2 us (3%)
    reduce_scatter x2, waiting for transfers between devices, body(): summed = lax.psum_scatter(partial, 'dev', scatter_dimension=0, tiled=True)  136 us
    all_gather x2, waiting for transfers between devices, body(): rows_in = lax.all_gather(normed, 'dev', axis=0, tiled=True)  57.3 us
    all_gather x1, blocking collectives, body(): weights = lax.all_gather(weights, 'dev', axis=1, tiled=True)  24.2 us
    dot_general x2, matrix products, run_expert(): projected = jnp.dot(rows_in, gate_up[0], preferred_element_type=jnp.float32)  20 us
    all_to_all x2, waiting for transfers between devices, body(): lax.all_to_all(outgoing_rows, 'dev', split_axis=1, concat_axis=1, tiled=T...  11.4 us
    all_to_all x2, starting transfers between devices, body(): lax.all_to_all(outgoing_rows, 'dev', split_axis=1, concat_axis=1, tiled=T...  11 us
    dot_general x2, matrix products, run_expert(): output = jnp.dot(hidden, down_proj[0], preferred_element_type=jnp.float32)  10.1 us
    dot_general x2, matrix products, attend(): jnp.einsum('mgqk,mkd->mqgd', weights, cached_pairs[:, 1], preferred_eleme...  8.07 us
  transfers between devices with their start and end apart: 6, of which 6 were waited for; matrix products, arithmetic and copies ran while one was open for 13% of the time, Pallas kernels for 0%

commit v1 on v0

--- a/solution.py
+++ b/solution.py
@@ -82,7 +82,14 @@
         arrived_rows = lax.all_to_all(outgoing_rows, "dev", split_axis=1, concat_axis=1, tiled=True)
         attn_rows = to_owners(arrived_rows, kv_heads)
         stream, normed = prepare(attn_rows[0], residual[batch_index], norm_gain)
-        rows_in = lax.all_gather(normed, "dev", axis=0, tiled=True)
+        ways = lax.axis_size("dev")
+        pieces_2 = [normed]
+        for far in range(1, ways):
+            pieces_2.append(
+                lax.ppermute(pieces_2[far - 1], "dev", [(d, (d - 1) % ways) for d in range(ways)])
+            )
+        line = jnp.concatenate(pieces_2, axis=0)
+        rows_in = jnp.roll(line, lax.axis_index("dev") * normed.shape[0], axis=0)
         partial = run_expert(rows_in, gate_up, down_proj, mine[batch_index])
         summed = lax.psum_scatter(partial, "dev", scatter_dimension=0, tiled=True)
         pieces.append((stream + summed.astype(jnp.float32)).astype(jnp.bfloat16))

time: 325 us -> 388 us (1.19)
  starting transfers between devices: 11.3 us -> 111 us
  waiting for transfers between devices: 205 us -> 126 us
  local copies, waits for them, and re-layouts: 15.7 us -> 53.3 us
    ppermute x0 -> x30, starting transfers between devices: none -> 97.9 us  [body(): lax.ppermute(pieces_2[far - 1], 'dev', [(d, (d - 1) % ways) for d in rang...]
    reduce_scatter x2, waiting for transfers between devices: 136 us -> 75.8 us  [body(): summed = lax.psum_scatter(partial, 'dev', scatter_dimension=0, tiled=True)]
    all_gather x2 -> x0, waiting for transfers between devices: 57.3 us -> none  [body(): rows_in = lax.all_gather(normed, 'dev', axis=0, tiled=True)]
    ppermute x0 -> x30, waiting for transfers between devices: none -> 41.9 us  [body(): lax.ppermute(pieces_2[far - 1], 'dev', [(d, (d - 1) % ways) for d in rang...]
    unnamed x20 -> x60, local copies, waits for them, and re-layouts: 6.13 us -> 43.4 us
  transfers between devices with their start and end apart: 6 -> 34, of which waited for: 6 -> 20; matrix products, arithmetic and copies ran while one was open for 13% -> 22% of each run, Pallas kernels for 0% -> 0%
where the time goes in v1:
time: 388 us; the launch traced here: 386 us
  waiting for transfers between devices  126 us (32%)
  starting transfers between devices  111 us (29%)
  local copies, waits for them, and re-layouts  53.3 us (14%)
  matrix products  44.2 us (11%)
  blocking collectives  23.8 us (6%)
  other arithmetic  14.3 us (4%)
  between operations  13.7 us (4%)
    ppermute x30, starting transfers between devices, body(): lax.ppermute(pieces_2[far - 1], 'dev', [(d, (d - 1) % ways) for d in rang...  97.9 us
    reduce_scatter x2, waiting for transfers between devices, body(): summed = lax.psum_scatter(partial, 'dev', scatter_dimension=0, tiled=True)  75.8 us
    unnamed x60, local copies, waits for them, and re-layouts  43.4 us
    ppermute x30, waiting for transfers between devices, body(): lax.ppermute(pieces_2[far - 1], 'dev', [(d, (d - 1) % ways) for d in rang...  41.9 us
    all_gather x1, blocking collectives, body(): weights = lax.all_gather(weights, 'dev', axis=1, tiled=True)  23.8 us
    dot_general x2, matrix products, run_expert(): projected = jnp.dot(rows_in, gate_up[0], preferred_element_type=jnp.float32)  20.8 us
    all_to_all x2, starting transfers between devices, body(): lax.all_to_all(outgoing_rows, 'dev', split_axis=1, concat_axis=1, tiled=T...  12.9 us
    dot_general x2, matrix products, run_expert(): output = jnp.dot(hidden, down_proj[0], preferred_element_type=jnp.float32)  10.3 us
  transfers between devices with their start and end apart: 34, of which 20 were waited for; matrix products, arithmetic and copies ran while one was open for 22% of the time, Pallas kernels for 0%

profile of v1, /device:TPU:0, one launch (start us, length us, event | category | flops | bytes accessed | tf_op | source)
XLA Modules:
  0.0 386.4 jit_solution(1999528252751871929)
XLA Ops:
  13.9 2.3 fusion.4
  16.2 4.6 %fusion.6 = (f32[8,128]{1,0:T(8,128)S(1)}, f32[8,128]{1,0:T(8,128)S(1)}, f32[1664,128,8]{1,0,2:T(8,128)}) fusion(f32[1664,128,8]{1,0,2:T(8,128)S(1)} %get-tuple-element.25, f32[8,128]{1,0:T(8,128)S(1)} %get-tuple-element.24, pred[128,1664]{0,1:T(8,128)(4,1)S(1)} %iota_compare_fusion, bf16[128,8,128]{0,2,1:T(8,128)(2,1)S(1)} %bitcast.158, ...), kind=kOutput, calls=%fused_computation.18 | convolution fusion | flops 449837056 | bytes 14544896 | tf_op jit(solution)/shard_map/mqgd,mkd->mgqk/dot_general | solution.py:14
  20.8 2.6 fusion.33
  26.0 7.5 %all-to-all-start = ((bf16[1,16,8,1024]{3,2,0,1:T(8,128)(2,1)}), bf16[1,16,8,1024]{3,2,0,1:T(8,128)(2,1)}, u32[]{:S(2)}, u32[]{:S(2)}) async-start(bf16[1,16,8,1024]{3,2,0,1:T(8,128)(2,1)} %bitcast.156), calls=%async_computation | async-start | bytes 524288 | tf_op jit(solution)/shard_map/all_to_all | solution.py:82
  33.5 4.7 %fusion.7 = f32[8,128]{1,0:T(8,128)S(1)} fusion(f32[1664,128,8]{1,0,2:T(8,128)} %get-tuple-element.26, f32[8,128]{1,0:T(8,128)S(1)} %get-tuple-element.9, pred[128,1664]{0,1:T(8,128)(4,1)S(1)} %iota_compare_fusion), kind=kLoop, calls=%fused_computation.19 | loop fusion | flops 8518656 | bytes 7036928 | tf_op jit(solution)/shard_map/reduce_sum | solution.py:23
  38.4 3.6 fusion.30
  43.6 5.4 %all-to-all-start.1 = ((bf16[1,16,8,1024]{3,2,0,1:T(8,128)(2,1)}), bf16[1,16,8,1024]{3,2,0,1:T(8,128)(2,1)S(1)}, u32[]{:S(2)}, u32[]{:S(2)}) async-start(bf16[1,16,8,1024]{3,2,0,1:T(8,128)(2,1)} %bitcast.157), calls=%async_computation.2 | async-start | bytes 524288 | tf_op jit(solution)/shard_map/all_to_all | solution.py:82
  50.9 8.1 %all-to-all-done.1 = bf16[1,16,8,1024]{3,2,0,1:T(8,128)(2,1)S(1)} async-done(((bf16[1,16,8,1024]{3,2,0,1:T(8,128)(2,1)}), bf16[1,16,8,1024]{3,2,0,1:T(8,128)(2,1)S(1)}, u32[]{:S(2)}, u32[]{:S(2)}) %all-to-all-start.1) | async-done | bytes 262176 | tf_op jit(solution)/shard_map/all_to_all | solution.py:82
  64.3 3.9 %collective-permute-done.15 = bf16[64,2048]{1,0:T(8,128)(2,1)S(1)} collective-permute-done((bf16[64,2048]{1,0:T(8,128)(2,1)S(1)}, bf16[64,2048]{1,0:T(8,128)(2,1)S(1)}, u32[]{:S(2)}, u32[]{:S(2)}) %collective-permute-start.15) | collective-permute-done | bytes 262176 | tf_op jit(solution)/shard_map/ppermute | solution.py:89
  68.1 4.6 %collective-permute-start.16 = (bf16[64,2048]{1,0:T(8,128)(2,1)S(1)}, bf16[64,2048]{1,0:T(8,128)(2,1)S(1)}, u32[]{:S(2)}, u32[]{:S(2)}) collective-permute-start(bf16[64,2048]{1,0:T(8,128)(2,1)S(1)} %collective-permute-done.15), channel_id=1, source_target_pairs={{0,15},{1,0},{2,1},{3,2},{4,3},{5,4},{6,5},{7,6},{8,7},{9,8},{10,9... | collective-permute-start | bytes 786440 | tf_op jit(solution)/shard_map/ppermute | solution.py:89
  72.8 3.9 %collective-permute-done.16 = bf16[64,2048]{1,0:T(8,128)(2,1)S(1)} collective-permute-done((bf16[64,2048]{1,0:T(8,128)(2,1)S(1)}, bf16[64,2048]{1,0:T(8,128)(2,1)S(1)}, u32[]{:S(2)}, u32[]{:S(2)}) %collective-permute-start.16) | collective-permute-done | bytes 262176 | tf_op jit(solution)/shard_map/ppermute | solution.py:89
  76.6 4.6 %collective-permute-start.17 = (bf16[64,2048]{1,0:T(8,128)(2,1)S(1)}, bf16[64,2048]{1,0:T(8,128)(2,1)S(1)}, u32[]{:S(2)}, u32[]{:S(2)}) collective-permute-start(bf16[64,2048]{1,0:T(8,128)(2,1)S(1)} %collective-permute-done.16), channel_id=1, source_target_pairs={{0,15},{1,0},{2,1},{3,2},{4,3},{5,4},{6,5},{7,6},{8,7},{9,8},{10,9... | collective-permute-start | bytes 786440 | tf_op jit(solution)/shard_map/ppermute | solution.py:89
  81.3 3.9 collective-permute-done.17
  85.1 4.6 %collective-permute-start.18 = (bf16[64,2048]{1,0:T(8,128)(2,1)S(1)}, bf16[64,2048]{1,0:T(8,128)(2,1)S(1)}, u32[]{:S(2)}, u32[]{:S(2)}) collective-permute-start(bf16[64,2048]{1,0:T(8,128)(2,1)S(1)} %collective-permute-done.17), channel_id=1, source_target_pairs={{0,15},{1,0},{2,1},{3,2},{4,3},{5,4},{6,5},{7,6},{8,7},{9,8},{10,9... | collective-permute-start | bytes 786440 | tf_op jit(solution)/shard_map/ppermute | solution.py:89
  89.7 2.8 collective-permute-start.1
  93.6 4.6 %collective-permute-start.19 = (bf16[64,2048]{1,0:T(8,128)(2,1)S(1)}, bf16[64,2048]{1,0:T(8,128)(2,1)}, u32[]{:S(2)}, u32[]{:S(2)}) collective-permute-start(bf16[64,2048]{1,0:T(8,128)(2,1)S(1)} %collective-permute-done.18), channel_id=1, source_target_pairs={{0,15},{1,0},{2,1},{3,2},{4,3},{5,4},{6,5},{7,6},{8,7},{9,8},{10,9... | collective-permute-start | bytes 786440 | tf_op jit(solution)/shard_map/ppermute | solution.py:89
  98.2 2.9 collective-permute-start.2
  102.1 4.7 %collective-permute-start.20 = (bf16[64,2048]{1,0:T(8,128)(2,1)}, bf16[64,2048]{1,0:T(8,128)(2,1)}, u32[]{:S(2)}, u32[]{:S(2)}) collective-permute-start(bf16[64,2048]{1,0:T(8,128)(2,1)} %collective-permute-done.19), channel_id=1, source_target_pairs={{0,15},{1,0},{2,1},{3,2},{4,3},{5,4},{6,5},{7,6},{8,7},{9,8},{10,9... | collective-permute-start | bytes 786440 | tf_op jit(solution)/shard_map/ppermute | solution.py:89
  107.0 2.9 collective-permute-start.3
  111.0 4.7 %collective-permute-start.21 = (bf16[64,2048]{1,0:T(8,128)(2,1)}, bf16[64,2048]{1,0:T(8,128)(2,1)}, u32[]{:S(2)}, u32[]{:S(2)}) collective-permute-start(bf16[64,2048]{1,0:T(8,128)(2,1)} %collective-permute-done.20), channel_id=1, source_target_pairs={{0,15},{1,0},{2,1},{3,2},{4,3},{5,4},{6,5},{7,6},{8,7},{9,8},{10,9... | collective-permute-start | bytes 786440 | tf_op jit(solution)/shard_map/ppermute | solution.py:89
  115.8 23.8 %all_gather.3 = f32[2,1024,16]{2,0,1:T(2,128)S(1)} all-gather(f32[2,64,16]{2,0,1:T(2,128)S(1)} %copy.50), channel_id=1, replica_groups=mesh['groups'=2,'dev'=16] {'dev'}, dimensions={1}, use_global_device_ids=true | all-gather | bytes 139264 | tf_op jit(solution)/shard_map/all_gather | solution.py:73
  144.5 3.4 collective-permute-done.22
  147.8 4.6 %collective-permute-start.23 = (bf16[64,2048]{1,0:T(8,128)(2,1)}, bf16[64,2048]{1,0:T(8,128)(2,1)S(1)}, u32[]{:S(2)}, u32[]{:S(2)}) collective-permute-start(bf16[64,2048]{1,0:T(8,128)(2,1)} %collective-permute-done.22), channel_id=1, source_target_pairs={{0,15},{1,0},{2,1},{3,2},{4,3},{5,4},{6,5},{7,6},{8,7},{9,8},{10,9... | collective-permute-start | bytes 786440 | tf_op jit(solution)/shard_map/ppermute | solution.py:89
  156.6 4.5 %collective-permute-start.24 = (bf16[64,2048]{1,0:T(8,128)(2,1)S(1)}, bf16[64,2048]{1,0:T(8,128)(2,1)S(1)}, u32[]{:S(2)}, u32[]{:S(2)}) collective-permute-start(bf16[64,2048]{1,0:T(8,128)(2,1)S(1)} %collective-permute-done.23), channel_id=1, source_target_pairs={{0,15},{1,0},{2,1},{3,2},{4,3},{5,4},{6,5},{7,6},{8,7},{9,8},{10,9... | collective-permute-start | bytes 786440 | tf_op jit(solution)/shard_map/ppermute | solution.py:89
  166.3 3.3 collective-permute-start.25
  175.5 2.6 collective-permute-start.26
  179.8 2.7 collective-permute-start.8
  184.1 2.5 collective-permute-start.27
  188.1 2.4 collective-permute-done.27
  190.5 4.6 %collective-permute-start.28 = (bf16[64,2048]{1,0:T(8,128)(2,1)S(1)}, bf16[64,2048]{1,0:T(8,128)(2,1)S(1)}, u32[]{:S(2)}, u32[]{:S(2)}) collective-permute-start(bf16[64,2048]{1,0:T(8,128)(2,1)S(1)} %collective-permute-done.27), channel_id=1, source_target_pairs={{0,15},{1,0},{2,1},{3,2},{4,3},{5,4},{6,5},{7,6},{8,7},{9,8},{10,9... | collective-permute-start | bytes 786440 | tf_op jit(solution)/shard_map/ppermute | solution.py:89
  196.5 2.4 collective-permute-done.28
  199.0 4.6 %collective-permute-start.29 = (bf16[64,2048]{1,0:T(8,128)(2,1)S(1)}, bf16[64,2048]{1,0:T(8,128)(2,1)S(1)}, u32[]{:S(2)}, u32[]{:S(2)}) collective-permute-start(bf16[64,2048]{1,0:T(8,128)(2,1)S(1)} %collective-permute-done.28), channel_id=1, source_target_pairs={{0,15},{1,0},{2,1},{3,2},{4,3},{5,4},{6,5},{7,6},{8,7},{9,8},{10,9... | collective-permute-start | bytes 786440 | tf_op jit(solution)/shard_map/ppermute | solution.py:89
  205.1 2.4 collective-permute-done.29
  208.2 10.3 %fusion = f32[1024,1536]{1,0:T(8,128)S(1)} fusion(bf16[1,2048,1536]{2,1,0:T(8,128)(2,1)} %param.14, s32[]{:T(128)S(6)} %select_n.40, bf16[1024,2048]{1,0:T(8,128)(2,1)} %constant_dynamic-update-slice_fusion.16), kind=kOutput, calls=%fused_computation.12 | convolution fusion | flops 6450839552 | bytes 16777220 | tf_op jit(solution)/shard_map/dot_general | solution.py:54
  218.6 5.2 %multiply_convert_fusion = bf16[1024,2048]{1,0:T(8,128)(2,1)} fusion(f32[1024]{0:T(1024)S(1)} %bitcast.160, bf16[1,768,2048]{2,1,0:T(8,128)(2,1)S(1)} %copy-done, f32[1024,1536]{1,0:T(8,128)S(1)} %fusion), kind=kOutput, calls=%fused_computation.4 | convolution fusion | flops 3230138368 | bytes 13635584 | tf_op jit(solution)/shard_map/dot_general | solution.py:58
  226.3 4.6 %collective-permute-start.9 = (bf16[64,2048]{1,0:T(8,128)(2,1)}, bf16[64,2048]{1,0:T(8,128)(2,1)S(1)}, u32[]{:S(2)}, u32[]{:S(2)}) collective-permute-start(bf16[64,2048]{1,0:T(8,128)(2,1)} %collective-permute-done.8), channel_id=1, source_target_pairs={{0,15},{1,0},{2,1},{3,2},{4,3},{5,4},{6,5},{7,6},{8,7},{9,8},{10,9... | collective-permute-start | bytes 786440 | tf_op jit(solution)/shard_map/ppermute | solution.py:89
  235.1 4.5 %collective-permute-start.10 = (bf16[64,2048]{1,0:T(8,128)(2,1)S(1)}, bf16[64,2048]{1,0:T(8,128)(2,1)S(1)}, u32[]{:S(2)}, u32[]{:S(2)}) collective-permute-start(bf16[64,2048]{1,0:T(8,128)(2,1)S(1)} %collective-permute-done.9), channel_id=1, source_target_pairs={{0,15},{1,0},{2,1},{3,2},{4,3},{5,4},{6,5},{7,6},{8,7},{9,8},{10,9... | collective-permute-start | bytes 786440 | tf_op jit(solution)/shard_map/ppermute | solution.py:89
  243.5 4.6 %collective-permute-start.11 = (bf16[64,2048]{1,0:T(8,128)(2,1)S(1)}, bf16[64,2048]{1,0:T(8,128)(2,1)S(1)}, u32[]{:S(2)}, u32[]{:S(2)}) collective-permute-start(bf16[64,2048]{1,0:T(8,128)(2,1)S(1)} %collective-permute-done.10), channel_id=1, source_target_pairs={{0,15},{1,0},{2,1},{3,2},{4,3},{5,4},{6,5},{7,6},{8,7},{9,8},{10,9... | collective-permute-start | bytes 786440 | tf_op jit(solution)/shard_map/ppermute | solution.py:89
  252.0 4.6 %collective-permute-start.12 = (bf16[64,2048]{1,0:T(8,128)(2,1)S(1)}, bf16[64,2048]{1,0:T(8,128)(2,1)S(1)}, u32[]{:S(2)}, u32[]{:S(2)}) collective-permute-start(bf16[64,2048]{1,0:T(8,128)(2,1)S(1)} %collective-permute-done.11), channel_id=1, source_target_pairs={{0,15},{1,0},{2,1},{3,2},{4,3},{5,4},{6,5},{7,6},{8,7},{9,8},{10,9... | collective-permute-start | bytes 786440 | tf_op jit(solution)/shard_map/ppermute | solution.py:89
  259.0 5.3 %collective-permute-done.12 = bf16[64,2048]{1,0:T(8,128)(2,1)S(1)} collective-permute-done((bf16[64,2048]{1,0:T(8,128)(2,1)S(1)}, bf16[64,2048]{1,0:T(8,128)(2,1)S(1)}, u32[]{:S(2)}, u32[]{:S(2)}) %collective-permute-start.12) | collective-permute-done | bytes 262176 | tf_op jit(solution)/shard_map/ppermute | solution.py:89
  264.3 4.7 %collective-permute-start.13 = (bf16[64,2048]{1,0:T(8,128)(2,1)S(1)}, bf16[64,2048]{1,0:T(8,128)(2,1)S(1)}, u32[]{:S(2)}, u32[]{:S(2)}) collective-permute-start(bf16[64,2048]{1,0:T(8,128)(2,1)S(1)} %collective-permute-done.12), channel_id=1, source_target_pairs={{0,15},{1,0},{2,1},{3,2},{4,3},{5,4},{6,5},{7,6},{8,7},{9,8},{10,9... | collective-permute-start | bytes 786440 | tf_op jit(solution)/shard_map/ppermute | solution.py:89
  270.5 6.0 %collective-permute-done.13 = bf16[64,2048]{1,0:T(8,128)(2,1)S(1)} collective-permute-done((bf16[64,2048]{1,0:T(8,128)(2,1)S(1)}, bf16[64,2048]{1,0:T(8,128)(2,1)S(1)}, u32[]{:S(2)}, u32[]{:S(2)}) %collective-permute-start.13) | collective-permute-done | bytes 262176 | tf_op jit(solution)/shard_map/ppermute | solution.py:89
  276.4 4.6 %collective-permute-start.14 = (bf16[64,2048]{1,0:T(8,128)(2,1)S(1)}, bf16[64,2048]{1,0:T(8,128)(2,1)S(1)}, u32[]{:S(2)}, u32[]{:S(2)}) collective-permute-start(bf16[64,2048]{1,0:T(8,128)(2,1)S(1)} %collective-permute-done.13), channel_id=1, source_target_pairs={{0,15},{1,0},{2,1},{3,2},{4,3},{5,4},{6,5},{7,6},{8,7},{9,8},{10,9... | collective-permute-start | bytes 786440 | tf_op jit(solution)/shard_map/ppermute | solution.py:89
  282.5 2.4 collective-permute-done.14
  285.7 10.5 %fusion.2 = f32[1024,1536]{1,0:T(8,128)S(1)} fusion(bf16[1,2048,1536]{2,1,0:T(8,128)(2,1)} %param.14, s32[]{:T(128)S(6)} %select_n.40, bf16[1024,2048]{1,0:T(8,128)(2,1)} %constant_dynamic-update-slice_fusion), kind=kOutput, calls=%fused_computation.14 | convolution fusion | flops 6450839552 | bytes 16777220 | tf_op jit(solution)/shard_map/dot_general | solution.py:54
  296.2 5.1 %multiply_convert_fusion.1 = bf16[1024,2048]{1,0:T(8,128)(2,1)} fusion(f32[1024]{0:T(1024)S(1)} %bitcast.159, bf16[1,768,2048]{2,1,0:T(8,128)(2,1)S(1)} %copy-done, f32[1024,1536]{1,0:T(8,128)S(1)} %fusion.2), kind=kOutput, calls=%fused_computation.5 | convolution fusion | flops 3230138368 | bytes 13635584 | tf_op jit(solution)/shard_map/dot_general | solution.py:58
  301.4 75.7 %reduce-scatter.3.cloned.1.call-done = bf16[64,2048]{1,0:T(8,128)(2,1)} async-done(((bf16[1024,2048]{1,0:T(8,128)(2,1)}), bf16[64,2048]{1,0:T(8,128)(2,1)}) %reduce-scatter.3.cloned.1.call-update) | async-done | bytes 262160 | tf_op jit(solution)/shard_map/reduce_scatter | solution.py:94
  377.1 2.5 fusion.38
  (115 shorter events, 71.3 us)
Async XLA Ops:
  6.5 212.0 %copy-start = (bf16[1,768,2048]{2,1,0:T(8,128)(2,1)S(1)}, bf16[1,768,2048]{2,1,0:T(8,128)(2,1)}, u32[]{:S(2)}) copy-start(bf16[1,768,2048]{2,1,0:T(8,128)(2,1)} %param.15) | copy-start | bytes 9437188
  13.8 2.3 copy-start.3
  13.8 2.3 copy-start.10
  26.0 17.5 %all-to-all-start = ((bf16[1,16,8,1024]{3,2,0,1:T(8,128)(2,1)}), bf16[1,16,8,1024]{3,2,0,1:T(8,128)(2,1)}, u32[]{:S(2)}, u32[]{:S(2)}) async-start(bf16[1,16,8,1024]{3,2,0,1:T(8,128)(2,1)} %bitcast.156), calls=%async_computation | async-start | bytes 524288 | tf_op jit(solution)/shard_map/all_to_all | solution.py:82
  33.5 4.9 %copy-start.2 = (f32[1664,128,8]{1,0,2:T(8,128)S(1)}, f32[1664,128,8]{1,0,2:T(8,128)}, u32[]{:S(2)}) copy-start(f32[1664,128,8]{1,0,2:T(8,128)} %get-tuple-element.26) | copy-start | bytes 20447236
  42.0 18.7 %copy-start.11 = (f32[2048]{0:T(1024)S(1)}, f32[2048]{0:T(1024)}, u32[]{:S(2)}) copy-start(f32[2048]{0:T(1024)} %param.13) | copy-start | bytes 24580
  42.0 64.9 %copy-start.13 = (s32[2,64,8]{1,2,0:T(8,128)S(1)}, s32[2,64,8]{1,2,0:T(8,128)}, u32[]{:S(2)}) copy-start(s32[2,64,8]{1,2,0:T(8,128)} %param.17) | copy-start | bytes 12292
  42.0 64.9 %copy-start.12 = (s32[2,64,8]{1,2,0:T(8,128)S(1)}, s32[2,64,8]{1,2,0:T(8,128)}, u32[]{:S(2)}) copy-start(s32[2,64,8]{1,2,0:T(8,128)} %param.16) | copy-start | bytes 12292
  43.6 15.4 %all-to-all-start.1 = ((bf16[1,16,8,1024]{3,2,0,1:T(8,128)(2,1)}), bf16[1,16,8,1024]{3,2,0,1:T(8,128)(2,1)S(1)}, u32[]{:S(2)}, u32[]{:S(2)}) async-start(bf16[1,16,8,1024]{3,2,0,1:T(8,128)(2,1)} %bitcast.157), calls=%async_computation.2 | async-start | bytes 524288 | tf_op jit(solution)/shard_map/all_to_all | solution.py:82
  49.0 252.4 %reduce-scatter.5.cloned.1.call-start = ((), (), s32[]{:S(2)}) async-start(), calls=%async_computation.5 | async-start | bytes 4456448 | tf_op jit(solution)/shard_map/reduce_scatter | solution.py:94
  59.0 1.6 copy-start.1
  62.9 5.3 %collective-permute-start.15 = (bf16[64,2048]{1,0:T(8,128)(2,1)S(1)}, bf16[64,2048]{1,0:T(8,128)(2,1)S(1)}, u32[]{:S(2)}, u32[]{:S(2)}) collective-permute-start(bf16[64,2048]{1,0:T(8,128)(2,1)S(1)} %get-tuple-element.17), channel_id=1, source_target_pairs={{0,15},{1,0},{2,1},{3,2},{4,3},{5,4},{6,5},{7,6},{8,7},{9,8},{10,9... | collective-permute-start | bytes 786440 | tf_op jit(solution)/shard_map/ppermute | solution.py:89
  68.1 4.6 %copy-start.7 = (bf16[64,2048]{1,0:T(8,128)(2,1)}, bf16[64,2048]{1,0:T(8,128)(2,1)S(1)}, u32[]{:S(2)}) copy-start(bf16[64,2048]{1,0:T(8,128)(2,1)S(1)} %collective-permute-done.15) | copy-start | bytes 786436
  68.1 8.5 %collective-permute-start.16 = (bf16[64,2048]{1,0:T(8,128)(2,1)S(1)}, bf16[64,2048]{1,0:T(8,128)(2,1)S(1)}, u32[]{:S(2)}, u32[]{:S(2)}) collective-permute-start(bf16[64,2048]{1,0:T(8,128)(2,1)S(1)} %collective-permute-done.15), channel_id=1, source_target_pairs={{0,15},{1,0},{2,1},{3,2},{4,3},{5,4},{6,5},{7,6},{8,7},{9,8},{10,9... | collective-permute-start | bytes 786440 | tf_op jit(solution)/shard_map/ppermute | solution.py:89
  76.6 4.6 %copy-start.6 = (bf16[64,2048]{1,0:T(8,128)(2,1)}, bf16[64,2048]{1,0:T(8,128)(2,1)S(1)}, u32[]{:S(2)}) copy-start(bf16[64,2048]{1,0:T(8,128)(2,1)S(1)} %collective-permute-done.16) | copy-start | bytes 786436
  76.6 8.5 %collective-permute-start.17 = (bf16[64,2048]{1,0:T(8,128)(2,1)S(1)}, bf16[64,2048]{1,0:T(8,128)(2,1)S(1)}, u32[]{:S(2)}, u32[]{:S(2)}) collective-permute-start(bf16[64,2048]{1,0:T(8,128)(2,1)S(1)} %collective-permute-done.16), channel_id=1, source_target_pairs={{0,15},{1,0},{2,1},{3,2},{4,3},{5,4},{6,5},{7,6},{8,7},{9,8},{10,9... | collective-permute-start | bytes 786440 | tf_op jit(solution)/shard_map/ppermute | solution.py:89
  81.2 8.5 %collective-permute-start = (bf16[64,2048]{1,0:T(8,128)(2,1)S(1)}, bf16[64,2048]{1,0:T(8,128)(2,1)S(1)}, u32[]{:S(2)}, u32[]{:S(2)}) collective-permute-start(bf16[64,2048]{1,0:T(8,128)(2,1)S(1)} %get-tuple-element.11), channel_id=1, source_target_pairs={{0,15},{1,0},{2,1},{3,2},{4,3},{5,4},{6,5},{7,6},{8,7},{9,8},{10,9... | collective-permute-start | bytes 786440 | tf_op jit(solution)/shard_map/ppermute | solution.py:89
  85.1 13.1 %copy-start.4 = (bf16[64,2048]{1,0:T(8,128)(2,1)}, bf16[64,2048]{1,0:T(8,128)(2,1)S(1)}, u32[]{:S(2)}) copy-start(bf16[64,2048]{1,0:T(8,128)(2,1)S(1)} %collective-permute-done.17) | copy-start | bytes 786436
  85.1 8.5 %collective-permute-start.18 = (bf16[64,2048]{1,0:T(8,128)(2,1)S(1)}, bf16[64,2048]{1,0:T(8,128)(2,1)S(1)}, u32[]{:S(2)}, u32[]{:S(2)}) collective-permute-start(bf16[64,2048]{1,0:T(8,128)(2,1)S(1)} %collective-permute-done.17), channel_id=1, source_target_pairs={{0,15},{1,0},{2,1},{3,2},{4,3},{5,4},{6,5},{7,6},{8,7},{9,8},{10,9... | collective-permute-start | bytes 786440 | tf_op jit(solution)/shard_map/ppermute | solution.py:89
  89.7 8.5 %collective-permute-start.1 = (bf16[64,2048]{1,0:T(8,128)(2,1)S(1)}, bf16[64,2048]{1,0:T(8,128)(2,1)}, u32[]{:S(2)}, u32[]{:S(2)}) collective-permute-start(bf16[64,2048]{1,0:T(8,128)(2,1)S(1)} %collective-permute-done), channel_id=1, source_target_pairs={{0,15},{1,0},{2,1},{3,2},{4,3},{5,4},{6,5},{7,6},{8,7},{9,8},{10,9... | collective-permute-start | bytes 786440 | tf_op jit(solution)/shard_map/ppermute | solution.py:89
  93.6 7.5 %copy-start.5 = (bf16[64,2048]{1,0:T(8,128)(2,1)}, bf16[64,2048]{1,0:T(8,128)(2,1)S(1)}, u32[]{:S(2)}) copy-start(bf16[64,2048]{1,0:T(8,128)(2,1)S(1)} %collective-permute-done.18) | copy-start | bytes 786436
  93.6 8.5 %collective-permute-start.19 = (bf16[64,2048]{1,0:T(8,128)(2,1)S(1)}, bf16[64,2048]{1,0:T(8,128)(2,1)}, u32[]{:S(2)}, u32[]{:S(2)}) collective-permute-start(bf16[64,2048]{1,0:T(8,128)(2,1)S(1)} %collective-permute-done.18), channel_id=1, source_target_pairs={{0,15},{1,0},{2,1},{3,2},{4,3},{5,4},{6,5},{7,6},{8,7},{9,8},{10,9... | collective-permute-start | bytes 786440 | tf_op jit(solution)/shard_map/ppermute | solution.py:89
  98.2 8.8 %collective-permute-start.2 = (bf16[64,2048]{1,0:T(8,128)(2,1)}, bf16[64,2048]{1,0:T(8,128)(2,1)}, u32[]{:S(2)}, u32[]{:S(2)}) collective-permute-start(bf16[64,2048]{1,0:T(8,128)(2,1)} %collective-permute-done.1), channel_id=1, source_target_pairs={{0,15},{1,0},{2,1},{3,2},{4,3},{5,4},{6,5},{7,6},{8,7},{9,8},{10,9... | collective-permute-start | bytes 786440 | tf_op jit(solution)/shard_map/ppermute | solution.py:89
  102.1 8.9 %collective-permute-start.20 = (bf16[64,2048]{1,0:T(8,128)(2,1)}, bf16[64,2048]{1,0:T(8,128)(2,1)}, u32[]{:S(2)}, u32[]{:S(2)}) collective-permute-start(bf16[64,2048]{1,0:T(8,128)(2,1)} %collective-permute-done.19), channel_id=1, source_target_pairs={{0,15},{1,0},{2,1},{3,2},{4,3},{5,4},{6,5},{7,6},{8,7},{9,8},{10,9... | collective-permute-start | bytes 786440 | tf_op jit(solution)/shard_map/ppermute | solution.py:89
  107.0 33.7 %collective-permute-start.3 = (bf16[64,2048]{1,0:T(8,128)(2,1)}, bf16[64,2048]{1,0:T(8,128)(2,1)}, u32[]{:S(2)}, u32[]{:S(2)}) collective-permute-start(bf16[64,2048]{1,0:T(8,128)(2,1)} %collective-permute-done.2), channel_id=1, source_target_pairs={{0,15},{1,0},{2,1},{3,2},{4,3},{5,4},{6,5},{7,6},{8,7},{9,8},{10,9... | collective-permute-start | bytes 786440 | tf_op jit(solution)/shard_map/ppermute | solution.py:89
  111.0 29.8 %collective-permute-start.21 = (bf16[64,2048]{1,0:T(8,128)(2,1)}, bf16[64,2048]{1,0:T(8,128)(2,1)}, u32[]{:S(2)}, u32[]{:S(2)}) collective-permute-start(bf16[64,2048]{1,0:T(8,128)(2,1)} %collective-permute-done.20), channel_id=1, source_target_pairs={{0,15},{1,0},{2,1},{3,2},{4,3},{5,4},{6,5},{7,6},{8,7},{9,8},{10,9... | collective-permute-start | bytes 786440 | tf_op jit(solution)/shard_map/ppermute | solution.py:89
  140.7 13.4 %collective-permute-start.4 = (bf16[64,2048]{1,0:T(8,128)(2,1)}, bf16[64,2048]{1,0:T(8,128)(2,1)}, u32[]{:S(2)}, u32[]{:S(2)}) collective-permute-start(bf16[64,2048]{1,0:T(8,128)(2,1)} %collective-permute-done.3), channel_id=1, source_target_pairs={{0,15},{1,0},{2,1},{3,2},{4,3},{5,4},{6,5},{7,6},{8,7},{9,8},{10,9... | collective-permute-start | bytes 786440 | tf_op jit(solution)/shard_map/ppermute | solution.py:89
  140.8 7.0 %collective-permute-start.22 = (bf16[64,2048]{1,0:T(8,128)(2,1)}, bf16[64,2048]{1,0:T(8,128)(2,1)}, u32[]{:S(2)}, u32[]{:S(2)}) collective-permute-start(bf16[64,2048]{1,0:T(8,128)(2,1)} %collective-permute-done.21), channel_id=1, source_target_pairs={{0,15},{1,0},{2,1},{3,2},{4,3},{5,4},{6,5},{7,6},{8,7},{9,8},{10,9... | collective-permute-start | bytes 786440 | tf_op jit(solution)/shard_map/ppermute | solution.py:89
  147.8 8.8 %collective-permute-start.23 = (bf16[64,2048]{1,0:T(8,128)(2,1)}, bf16[64,2048]{1,0:T(8,128)(2,1)S(1)}, u32[]{:S(2)}, u32[]{:S(2)}) collective-permute-start(bf16[64,2048]{1,0:T(8,128)(2,1)} %collective-permute-done.22), channel_id=1, source_target_pairs={{0,15},{1,0},{2,1},{3,2},{4,3},{5,4},{6,5},{7,6},{8,7},{9,8},{10,9... | collective-permute-start | bytes 786440 | tf_op jit(solution)/shard_map/ppermute | solution.py:89
  154.1 8.7 %collective-permute-start.5 = (bf16[64,2048]{1,0:T(8,128)(2,1)}, bf16[64,2048]{1,0:T(8,128)(2,1)S(1)}, u32[]{:S(2)}, u32[]{:S(2)}) collective-permute-start(bf16[64,2048]{1,0:T(8,128)(2,1)} %collective-permute-done.4), channel_id=1, source_target_pairs={{0,15},{1,0},{2,1},{3,2},{4,3},{5,4},{6,5},{7,6},{8,7},{9,8},{10,9... | collective-permute-start | bytes 786440 | tf_op jit(solution)/shard_map/ppermute | solution.py:89
  156.6 9.7 %collective-permute-start.24 = (bf16[64,2048]{1,0:T(8,128)(2,1)S(1)}, bf16[64,2048]{1,0:T(8,128)(2,1)S(1)}, u32[]{:S(2)}, u32[]{:S(2)}) collective-permute-start(bf16[64,2048]{1,0:T(8,128)(2,1)S(1)} %collective-permute-done.23), channel_id=1, source_target_pairs={{0,15},{1,0},{2,1},{3,2},{4,3},{5,4},{6,5},{7,6},{8,7},{9,8},{10,9... | collective-permute-start | bytes 786440 | tf_op jit(solution)/shard_map/ppermute | solution.py:89
  162.8 0.7 copy-start.8
  163.5 7.8 %collective-permute-start.6 = (bf16[64,2048]{1,0:T(8,128)(2,1)S(1)}, bf16[64,2048]{1,0:T(8,128)(2,1)S(1)}, u32[]{:S(2)}, u32[]{:S(2)}) collective-permute-start(bf16[64,2048]{1,0:T(8,128)(2,1)S(1)} %collective-permute-done.5), channel_id=1, source_target_pairs={{0,15},{1,0},{2,1},{3,2},{4,3},{5,4},{6,5},{7,6},{8,7},{9,8},{10,9... | collective-permute-start | bytes 786440 | tf_op jit(solution)/shard_map/ppermute | solution.py:89
  166.3 9.2 %collective-permute-start.25 = (bf16[64,2048]{1,0:T(8,128)(2,1)S(1)}, bf16[64,2048]{1,0:T(8,128)(2,1)S(1)}, u32[]{:S(2)}, u32[]{:S(2)}) collective-permute-start(bf16[64,2048]{1,0:T(8,128)(2,1)S(1)} %collective-permute-done.24), channel_id=1, source_target_pairs={{0,15},{1,0},{2,1},{3,2},{4,3},{5,4},{6,5},{7,6},{8,7},{9,8},{10,9... | collective-permute-start | bytes 786440 | tf_op jit(solution)/shard_map/ppermute | solution.py:89
  171.3 0.7 copy-start.9
  172.0 7.8 %collective-permute-start.7 = (bf16[64,2048]{1,0:T(8,128)(2,1)S(1)}, bf16[64,2048]{1,0:T(8,128)(2,1)}, u32[]{:S(2)}, u32[]{:S(2)}) collective-permute-start(bf16[64,2048]{1,0:T(8,128)(2,1)S(1)} %collective-permute-done.6), channel_id=1, source_target_pairs={{0,15},{1,0},{2,1},{3,2},{4,3},{5,4},{6,5},{7,6},{8,7},{9,8},{10,9... | collective-permute-start | bytes 786440 | tf_op jit(solution)/shard_map/ppermute | solution.py:89
  175.5 8.6 %collective-permute-start.26 = (bf16[64,2048]{1,0:T(8,128)(2,1)S(1)}, bf16[64,2048]{1,0:T(8,128)(2,1)S(1)}, u32[]{:S(2)}, u32[]{:S(2)}) collective-permute-start(bf16[64,2048]{1,0:T(8,128)(2,1)S(1)} %collective-permute-done.25), channel_id=1, source_target_pairs={{0,15},{1,0},{2,1},{3,2},{4,3},{5,4},{6,5},{7,6},{8,7},{9,8},{10,9... | collective-permute-start | bytes 786440 | tf_op jit(solution)/shard_map/ppermute | solution.py:89
  179.8 46.5 %collective-permute-start.8 = (bf16[64,2048]{1,0:T(8,128)(2,1)}, bf16[64,2048]{1,0:T(8,128)(2,1)}, u32[]{:S(2)}, u32[]{:S(2)}) collective-permute-start(bf16[64,2048]{1,0:T(8,128)(2,1)} %collective-permute-done.7), channel_id=1, source_target_pairs={{0,15},{1,0},{2,1},{3,2},{4,3},{5,4},{6,5},{7,6},{8,7},{9,8},{10,9... | collective-permute-start | bytes 786440 | tf_op jit(solution)/shard_map/ppermute | solution.py:89
  184.1 6.4 %collective-permute-start.27 = (bf16[64,2048]{1,0:T(8,128)(2,1)S(1)}, bf16[64,2048]{1,0:T(8,128)(2,1)S(1)}, u32[]{:S(2)}, u32[]{:S(2)}) collective-permute-start(bf16[64,2048]{1,0:T(8,128)(2,1)S(1)} %collective-permute-done.26), channel_id=1, source_target_pairs={{0,15},{1,0},{2,1},{3,2},{4,3},{5,4},{6,5},{7,6},{8,7},{9,8},{10,9... | collective-permute-start | bytes 786440 | tf_op jit(solution)/shard_map/ppermute | solution.py:89
  190.5 8.5 %collective-permute-start.28 = (bf16[64,2048]{1,0:T(8,128)(2,1)S(1)}, bf16[64,2048]{1,0:T(8,128)(2,1)S(1)}, u32[]{:S(2)}, u32[]{:S(2)}) collective-permute-start(bf16[64,2048]{1,0:T(8,128)(2,1)S(1)} %collective-permute-done.27), channel_id=1, source_target_pairs={{0,15},{1,0},{2,1},{3,2},{4,3},{5,4},{6,5},{7,6},{8,7},{9,8},{10,9... | collective-permute-start | bytes 786440 | tf_op jit(solution)/shard_map/ppermute | solution.py:89
  199.0 8.5 %collective-permute-start.29 = (bf16[64,2048]{1,0:T(8,128)(2,1)S(1)}, bf16[64,2048]{1,0:T(8,128)(2,1)S(1)}, u32[]{:S(2)}, u32[]{:S(2)}) collective-permute-start(bf16[64,2048]{1,0:T(8,128)(2,1)S(1)} %collective-permute-done.28), channel_id=1, source_target_pairs={{0,15},{1,0},{2,1},{3,2},{4,3},{5,4},{6,5},{7,6},{8,7},{9,8},{10,9... | collective-permute-start | bytes 786440 | tf_op jit(solution)/shard_map/ppermute | solution.py:89
  223.8 153.3 %reduce-scatter.3.cloned.1.call-start = ((), (), s32[]{:S(2)}) async-start(), calls=%async_computation.4 | async-start | bytes 4456448 | tf_op jit(solution)/shard_map/reduce_scatter | solution.py:94
  226.3 8.8 %collective-permute-start.9 = (bf16[64,2048]{1,0:T(8,128)(2,1)}, bf16[64,2048]{1,0:T(8,128)(2,1)S(1)}, u32[]{:S(2)}, u32[]{:S(2)}) collective-permute-start(bf16[64,2048]{1,0:T(8,128)(2,1)} %collective-permute-done.8), channel_id=1, source_target_pairs={{0,15},{1,0},{2,1},{3,2},{4,3},{5,4},{6,5},{7,6},{8,7},{9,8},{10,9... | collective-permute-start | bytes 786440 | tf_op jit(solution)/shard_map/ppermute | solution.py:89
  235.1 8.4 %collective-permute-start.10 = (bf16[64,2048]{1,0:T(8,128)(2,1)S(1)}, bf16[64,2048]{1,0:T(8,128)(2,1)S(1)}, u32[]{:S(2)}, u32[]{:S(2)}) collective-permute-start(bf16[64,2048]{1,0:T(8,128)(2,1)S(1)} %collective-permute-done.9), channel_id=1, source_target_pairs={{0,15},{1,0},{2,1},{3,2},{4,3},{5,4},{6,5},{7,6},{8,7},{9,8},{10,9... | collective-permute-start | bytes 786440 | tf_op jit(solution)/shard_map/ppermute | solution.py:89
  243.5 8.5 %collective-permute-start.11 = (bf16[64,2048]{1,0:T(8,128)(2,1)S(1)}, bf16[64,2048]{1,0:T(8,128)(2,1)S(1)}, u32[]{:S(2)}, u32[]{:S(2)}) collective-permute-start(bf16[64,2048]{1,0:T(8,128)(2,1)S(1)} %collective-permute-done.10), channel_id=1, source_target_pairs={{0,15},{1,0},{2,1},{3,2},{4,3},{5,4},{6,5},{7,6},{8,7},{9,8},{10,9... | collective-permute-start | bytes 786440 | tf_op jit(solution)/shard_map/ppermute | solution.py:89
  252.0 12.4 %collective-permute-start.12 = (bf16[64,2048]{1,0:T(8,128)(2,1)S(1)}, bf16[64,2048]{1,0:T(8,128)(2,1)S(1)}, u32[]{:S(2)}, u32[]{:S(2)}) collective-permute-start(bf16[64,2048]{1,0:T(8,128)(2,1)S(1)} %collective-permute-done.11), channel_id=1, source_target_pairs={{0,15},{1,0},{2,1},{3,2},{4,3},{5,4},{6,5},{7,6},{8,7},{9,8},{10,9... | collective-permute-start | bytes 786440 | tf_op jit(solution)/shard_map/ppermute | solution.py:89
  264.3 12.1 %collective-permute-start.13 = (bf16[64,2048]{1,0:T(8,128)(2,1)S(1)}, bf16[64,2048]{1,0:T(8,128)(2,1)S(1)}, u32[]{:S(2)}, u32[]{:S(2)}) collective-permute-start(bf16[64,2048]{1,0:T(8,128)(2,1)S(1)} %collective-permute-done.12), channel_id=1, source_target_pairs={{0,15},{1,0},{2,1},{3,2},{4,3},{5,4},{6,5},{7,6},{8,7},{9,8},{10,9... | collective-permute-start | bytes 786440 | tf_op jit(solution)/shard_map/ppermute | solution.py:89
  276.4 8.5 %collective-permute-start.14 = (bf16[64,2048]{1,0:T(8,128)(2,1)S(1)}, bf16[64,2048]{1,0:T(8,128)(2,1)S(1)}, u32[]{:S(2)}, u32[]{:S(2)}) collective-permute-start(bf16[64,2048]{1,0:T(8,128)(2,1)S(1)} %collective-permute-done.13), channel_id=1, source_target_pairs={{0,15},{1,0},{2,1},{3,2},{4,3},{5,4},{6,5},{7,6},{8,7},{9,8},{10,9... | collective-permute-start | bytes 786440 | tf_op jit(solution)/shard_map/ppermute | solution.py:89
Sparse Core Ops, SparseCore 0:
  223.9 77.4 reduce-scatter.4
  305.2 71.8 reduce-scatter.2
